TPU v7x, 256 devices: a whole 4x4x8 slice. The times are simulated.
256 devices in a mesh: blk: 16 (over y, x_hi, core), uly: 16 (over z, x_lo).
Axes of the slice: x: 4 (x_hi: 2, x_lo: 2; x = x_hi * 2 + x_lo), y: 4, z: 8, core: 2. Of those that a mesh axis runs over, the one named last changes fastest.
Arguments:
- queries: bfloat16 [65536, 4096], P(('blk', 'uly')), may hold values from -6 to 6
- keys: bfloat16 [65536, 4096], P(('blk', 'uly')), may hold values from -6 to 6
- values: bfloat16 [65536, 4096], P(('blk', 'uly')), may hold values from -6 to 6
- doc_start: int32 [65536], P('blk'), may hold values from 0 to 65535, as said below
Outputs:
- attended: bfloat16 [65536, 4096], P(('blk', 'uly'))
Inputs may be any that keep to these rules, and one draw needn't show every extreme that they name: doc_start[0] = 0, and for t > 0 doc_start[t] is either t or doc_start[t - 1].
All inputs are finite; a program needn't handle non-finite values.
Results may differ from a plain program's by a relative error of at most 0.0026.
Values may be sent and summed in bfloat16 or wider, within the bound.
A program may use at most 128 MiB of HBM per device.

v0:
```python
import math
import jax
import jax.numpy as jnp
from jax import lax
from jax.sharding import PartitionSpec as P

HEAD_DIM = 128


def shifted(block, axis, distance):
    devices = range(lax.axis_size(axis))
    route = [(i - distance, i) for i in devices if i - distance in devices]
    return lax.ppermute(block, axis, route)


def previous_rows(key_stretch, value_stretch, window):
    key_prior, value_prior = shifted((key_stretch, value_stretch), "blk", 1)
    return (key_prior[-window:], value_prior[-window:])


def shards(queries, keys, values, doc_start):
    stretch_len = doc_start.shape[0]
    window = stretch_len // 2
    qblock = min(512, stretch_len)
    query_stretch, key_stretch, value_stretch = (
        lax.all_to_all(queries, "uly", split_axis=1, concat_axis=0, tiled=True),
        lax.all_to_all(keys, "uly", split_axis=1, concat_axis=0, tiled=True),
        lax.all_to_all(values, "uly", split_axis=1, concat_axis=0, tiled=True),
    )
    key_prior, value_prior = previous_rows(key_stretch, value_stretch, window)
    group_width = query_stretch.shape[1]
    group_heads = group_width // HEAD_DIM
    query_all = query_stretch.reshape(stretch_len, group_heads, HEAD_DIM)
    keys_wide = jnp.concatenate([key_prior, key_stretch], axis=0).reshape(
        stretch_len + window, group_heads, HEAD_DIM
    )
    values_wide = jnp.concatenate([value_prior, value_stretch], axis=0).reshape(
        stretch_len + window, group_heads, HEAD_DIM
    )
    anchor = lax.axis_index("blk") * stretch_len
    score_scale = 1.0 / math.sqrt(HEAD_DIM)

    def attend_span(first, query_rows, starts, skipped):
        span_len = qblock + window - skipped
        key_rows = lax.dynamic_slice_in_dim(keys_wide, first + skipped, span_len, 0)
        value_rows = lax.dynamic_slice_in_dim(values_wide, first + skipped, span_len, 0)
        query_pos = anchor + first + jnp.arange(qblock, dtype=jnp.int32)
        key_pos = anchor + first - window + skipped + jnp.arange(span_len, dtype=jnp.int32)
        allowed = (
            (key_pos[None, :] <= query_pos[:, None])
            & (key_pos[None, :] > query_pos[:, None] - window)
            & (key_pos[None, :] >= starts[:, None])
        )
        scores = (
            jnp.einsum("qhd,khd->hqk", query_rows, key_rows, preferred_element_type=jnp.float32)
            * score_scale
        )
        scores = jnp.where(allowed[None], scores, -jnp.inf)
        row_max = jnp.max(scores, axis=-1, keepdims=True)
        probs = jnp.exp(scores - row_max)
        totals = jnp.sum(probs, axis=-1)
        weights = probs.astype(jnp.bfloat16)
        mixed = jnp.einsum("hqk,khd->qhd", weights, value_rows, preferred_element_type=jnp.float32)
        mixed = mixed / jnp.transpose(totals)[:, :, None]
        return mixed.astype(jnp.bfloat16).reshape(qblock, group_width)

    def attend_block(block_index):
        first = block_index * qblock
        query_rows = lax.dynamic_slice_in_dim(query_all, first, qblock, 0)
        starts = lax.dynamic_slice_in_dim(doc_start, first, qblock, 0)
        return attend_span(first, query_rows, starts, 0)

    blocks = lax.map(attend_block, jnp.arange(stretch_len // qblock, dtype=jnp.int32))
    result = blocks.reshape(stretch_len, group_width)
    return lax.all_to_all(result, "uly", split_axis=0, concat_axis=1, tiled=True)


def solution(mesh):
    return jax.shard_map(
        shards,
        mesh=mesh,
        in_specs=(
            P(("blk", "uly"), None),
            P(("blk", "uly"), None),
            P(("blk", "uly"), None),
            P("blk"),
        ),
        out_specs=P(("blk", "uly"), None),
        check_vma=False,
    )
```

profile of v0, /device:TPU:12, one launch (start us, length us, event | category | flops | bytes accessed | tf_op | source)
XLA Modules:
  0.0 401.5 jit_solution(1465605567269902277)
XLA Ops:
  0.0 4.1 %copy.42 = bf16[256,4096]{0,1:T(8,128)(2,1)} copy(bf16[256,4096]{1,0:T(8,128)(2,1)} %param.7) | data formatting | bytes 4194304 | tf_op args[1]
  4.1 9.2 %all-to-all-start.2 = ((bf16[256,16,256]{0,2,1:T(8,128)(2,1)}), bf16[256,16,256]{0,2,1:T(8,128)(2,1)S(1)}, u32[]{:S(2)}, u32[]{:S(2)}) async-start(bf16[256,16,256]{0,2,1:T(8,128)(2,1)} %bitcast.42), calls=%async_computation.2 | async-start | bytes 4194304 | tf_op jit(solution)/shard_map/all_to_all | solution.py:27
  13.3 4.1 %copy.36 = bf16[256,4096]{0,1:T(8,128)(2,1)} copy(bf16[256,4096]{1,0:T(8,128)(2,1)} %param.8) | data formatting | bytes 4194304 | tf_op args[2]
  17.4 46.5 %all-to-all-done.2 = bf16[256,16,256]{0,2,1:T(8,128)(2,1)S(1)} async-done(((bf16[256,16,256]{0,2,1:T(8,128)(2,1)}), bf16[256,16,256]{0,2,1:T(8,128)(2,1)S(1)}, u32[]{:S(2)}, u32[]{:S(2)}) %all-to-all-start.2) | async-done | bytes 2097184 | tf_op jit(solution)/shard_map/all_to_all | solution.py:27
  63.8 4.4 %all-to-all-start = ((bf16[256,16,256]{0,2,1:T(8,128)(2,1)}), bf16[256,16,256]{0,2,1:T(8,128)(2,1)}, u32[]{:S(2)}, u32[]{:S(2)}) async-start(bf16[256,16,256]{0,2,1:T(8,128)(2,1)} %bitcast.41), calls=%async_computation | async-start | bytes 4194304 | tf_op jit(solution)/shard_map/all_to_all | solution.py:28
  68.3 4.1 %copy.40 = bf16[256,4096]{0,1:T(8,128)(2,1)} copy(bf16[256,4096]{1,0:T(8,128)(2,1)} %param.6) | data formatting | bytes 4194304 | tf_op args[0]
  72.4 45.6 %all-to-all-done = bf16[256,16,256]{0,2,1:T(8,128)(2,1)} async-done(((bf16[256,16,256]{0,2,1:T(8,128)(2,1)}), bf16[256,16,256]{0,2,1:T(8,128)(2,1)}, u32[]{:S(2)}, u32[]{:S(2)}) %all-to-all-start) | async-done | bytes 2097184 | tf_op jit(solution)/shard_map/all_to_all | solution.py:28
  118.0 4.4 %all-to-all-start.1 = ((bf16[256,16,256]{0,2,1:T(8,128)(2,1)}), bf16[256,16,256]{0,2,1:T(8,128)(2,1)}, u32[]{:S(2)}, u32[]{:S(2)}) async-start(bf16[256,16,256]{0,2,1:T(8,128)(2,1)} %bitcast.40), calls=%async_computation.1 | async-start | bytes 4194304 | tf_op jit(solution)/shard_map/all_to_all | solution.py:26
  137.0 4.1 %copy.38 = bf16[16,256,256]{1,0,2:T(8,128)(2,1)} copy(bf16[16,256,256]{1,2,0:T(8,128)(2,1)} %bitcast.8) | data formatting | bytes 4194304 | tf_op jit(solution)/shard_map/all_to_all | solution.py:28
  141.1 4.3 %concatenate.17 = bf16[4096,2,128]{0,2,1:T(8,128)(2,1)} reshape(bf16[16,256,256]{1,0,2:T(8,128)(2,1)} %copy.38) | data formatting | bytes 4194304 | tf_op jit(solution)/shard_map/concatenate | solution.py:37
  147.8 24.5 %all-to-all-done.1 = bf16[256,16,256]{0,2,1:T(8,128)(2,1)} async-done(((bf16[256,16,256]{0,2,1:T(8,128)(2,1)}), bf16[256,16,256]{0,2,1:T(8,128)(2,1)}, u32[]{:S(2)}, u32[]{:S(2)}) %all-to-all-start.1) | async-done | bytes 2097184 | tf_op jit(solution)/shard_map/all_to_all | solution.py:26
  179.4 16.7 %collective-permute-done = bf16[4096,256]{1,0:T(8,128)(2,1)} collective-permute-done((bf16[4096,256]{1,0:T(8,128)(2,1)}, bf16[4096,256]{1,0:T(8,128)(2,1)}, u32[]{:S(2)}, u32[]{:S(2)}) %collective-permute-start) | collective-permute-done | bytes 2097184 | tf_op jit(solution)/shard_map/ppermute | solution.py:13
  200.7 4.3 %pad_maximum_fusion = (bf16[6144,2,128]{0,2,1:T(8,128)(2,1)}, bf16[6144,2,128]{0,2,1:T(8,128)(2,1)}) fusion(bf16[4096,2,128]{0,2,1:T(8,128)(2,1)S(1)} %copy-done.1, bf16[2048,2,128]{0,2,1:T(8,128)(2,1)} %bitcast.47, bf16[4096,2,128]{0,2,1:T(8,128)(2,1)} %concatenate.20, bf16[2048,2,128]{0,2,1:T(8,128)(2,1)S(1)} %bitcast.46), kind=kLoop, calls=%fused_computation.23 | loop fusion | flops 12582912 | bytes 12582912 | tf_op jit(solution)/shard_map/concatenate | solution.py:37
  205.0 132.3 %while.13 = (s32[]{:T(128)}, bf16[8,512,256]{2,1,0:T(8,128)(2,1)}, s32[8]{0:T(128)S(1)}, bf16[6144,2,128]{0,2,1:T(8,128)(2,1)}, s32[]{:T(128)}, /*index=5*/s32[4...) while((s32[]{:T(128)}, bf16[8,512,256]{2,1,0:T(8,128)(2,1)}, ...), condition=%wide.region_3.4_spmd, body=%wide.region_0.3_spmd.sunk | while | flops 1377830400 | bytes 40950536 | solution.py:73
  216.0 4.6 %fusion.38 = bf16[512,2,128]{0,2,1:T(8,128)(2,1)S(1)} fusion(f32[2,512,2560]{2,1,0:T(8,128)S(1)} %get-tuple-element.238, f32[2,512]{1,0:T(2,128)S(1)} %get-tuple-element.239, pred[512,2560]{1,0:T(8,128)(4,1)S(1)} %compare_and_fusion.2, bf16[6144,2,128]{0,2,1:T(8,128)(2,1)} %get-tuple-element.271, s32[]{:T(128)S(6)} %select_n.49, ...), kind=kOutput, calls=%fused_computation.13.clone.1 | convolution fusion | flops 681836544 | bytes 13377540 | tf_op jit(solution)/shard_map/while/body/eval_jaxpr/hqk,khd->qhd/dot_general | solution.py:63
  232.6 4.6 %fusion.38 = bf16[512,2,128]{0,2,1:T(8,128)(2,1)S(1)} fusion(f32[2,512,2560]{2,1,0:T(8,128)S(1)} %get-tuple-element.238, f32[2,512]{1,0:T(2,128)S(1)} %get-tuple-element.239, pred[512,2560]{1,0:T(8,128)(4,1)S(1)} %compare_and_fusion.2, bf16[6144,2,128]{0,2,1:T(8,128)(2,1)} %get-tuple-element.271, s32[]{:T(128)S(6)} %select_n.49, ...), kind=kOutput, calls=%fused_computation.13.clone.1 | convolution fusion | flops 681836544 | bytes 13377540 | tf_op jit(solution)/shard_map/while/body/eval_jaxpr/hqk,khd->qhd/dot_general | solution.py:63
  249.1 4.6 %fusion.38 = bf16[512,2,128]{0,2,1:T(8,128)(2,1)S(1)} fusion(f32[2,512,2560]{2,1,0:T(8,128)S(1)} %get-tuple-element.238, f32[2,512]{1,0:T(2,128)S(1)} %get-tuple-element.239, pred[512,2560]{1,0:T(8,128)(4,1)S(1)} %compare_and_fusion.2, bf16[6144,2,128]{0,2,1:T(8,128)(2,1)} %get-tuple-element.271, s32[]{:T(128)S(6)} %select_n.49, ...), kind=kOutput, calls=%fused_computation.13.clone.1 | convolution fusion | flops 681836544 | bytes 13377540 | tf_op jit(solution)/shard_map/while/body/eval_jaxpr/hqk,khd->qhd/dot_general | solution.py:63
  265.6 4.6 %fusion.38 = bf16[512,2,128]{0,2,1:T(8,128)(2,1)S(1)} fusion(f32[2,512,2560]{2,1,0:T(8,128)S(1)} %get-tuple-element.238, f32[2,512]{1,0:T(2,128)S(1)} %get-tuple-element.239, pred[512,2560]{1,0:T(8,128)(4,1)S(1)} %compare_and_fusion.2, bf16[6144,2,128]{0,2,1:T(8,128)(2,1)} %get-tuple-element.271, s32[]{:T(128)S(6)} %select_n.49, ...), kind=kOutput, calls=%fused_computation.13.clone.1 | convolution fusion | flops 681836544 | bytes 13377540 | tf_op jit(solution)/shard_map/while/body/eval_jaxpr/hqk,khd->qhd/dot_general | solution.py:63
  282.2 4.6 %fusion.38 = bf16[512,2,128]{0,2,1:T(8,128)(2,1)S(1)} fusion(f32[2,512,2560]{2,1,0:T(8,128)S(1)} %get-tuple-element.238, f32[2,512]{1,0:T(2,128)S(1)} %get-tuple-element.239, pred[512,2560]{1,0:T(8,128)(4,1)S(1)} %compare_and_fusion.2, bf16[6144,2,128]{0,2,1:T(8,128)(2,1)} %get-tuple-element.271, s32[]{:T(128)S(6)} %select_n.49, ...), kind=kOutput, calls=%fused_computation.13.clone.1 | convolution fusion | flops 681836544 | bytes 13377540 | tf_op jit(solution)/shard_map/while/body/eval_jaxpr/hqk,khd->qhd/dot_general | solution.py:63
  298.7 4.6 %fusion.38 = bf16[512,2,128]{0,2,1:T(8,128)(2,1)S(1)} fusion(f32[2,512,2560]{2,1,0:T(8,128)S(1)} %get-tuple-element.238, f32[2,512]{1,0:T(2,128)S(1)} %get-tuple-element.239, pred[512,2560]{1,0:T(8,128)(4,1)S(1)} %compare_and_fusion.2, bf16[6144,2,128]{0,2,1:T(8,128)(2,1)} %get-tuple-element.271, s32[]{:T(128)S(6)} %select_n.49, ...), kind=kOutput, calls=%fused_computation.13.clone.1 | convolution fusion | flops 681836544 | bytes 13377540 | tf_op jit(solution)/shard_map/while/body/eval_jaxpr/hqk,khd->qhd/dot_general | solution.py:63
  315.3 4.6 %fusion.38 = bf16[512,2,128]{0,2,1:T(8,128)(2,1)S(1)} fusion(f32[2,512,2560]{2,1,0:T(8,128)S(1)} %get-tuple-element.238, f32[2,512]{1,0:T(2,128)S(1)} %get-tuple-element.239, pred[512,2560]{1,0:T(8,128)(4,1)S(1)} %compare_and_fusion.2, bf16[6144,2,128]{0,2,1:T(8,128)(2,1)} %get-tuple-element.271, s32[]{:T(128)S(6)} %select_n.49, ...), kind=kOutput, calls=%fused_computation.13.clone.1 | convolution fusion | flops 681836544 | bytes 13377540 | tf_op jit(solution)/shard_map/while/body/eval_jaxpr/hqk,khd->qhd/dot_general | solution.py:63
  331.8 4.6 %fusion.38 = bf16[512,2,128]{0,2,1:T(8,128)(2,1)S(1)} fusion(f32[2,512,2560]{2,1,0:T(8,128)S(1)} %get-tuple-element.238, f32[2,512]{1,0:T(2,128)S(1)} %get-tuple-element.239, pred[512,2560]{1,0:T(8,128)(4,1)S(1)} %compare_and_fusion.2, bf16[6144,2,128]{0,2,1:T(8,128)(2,1)} %get-tuple-element.271, s32[]{:T(128)S(6)} %select_n.49, ...), kind=kOutput, calls=%fused_computation.13.clone.1 | convolution fusion | flops 681836544 | bytes 13377540 | tf_op jit(solution)/shard_map/while/body/eval_jaxpr/hqk,khd->qhd/dot_general | solution.py:63
  337.3 57.8 %all_to_all.73 = bf16[16,256,256]{2,1,0:T(8,128)(2,1)S(1)} all-to-all(bf16[16,256,256]{2,1,0:T(8,128)(2,1)} %bitcast.48), channel_id=1, replica_groups=mesh['blk'=16,'uly'=16] {'uly'}, dimensions={0} | all-to-all | bytes 4194304 | tf_op jit(solution)/shard_map/all_to_all | solution.py:75
  397.4 4.1 %copy.50 = bf16[256,4096]{1,0:T(8,128)(2,1)} copy(bf16[256,4096]{0,1:T(8,128)(2,1)} %bitcast.44) | data formatting | bytes 4194304 | tf_op jit(solution)/shard_map/all_to_all | solution.py:75
  (92 shorter events, 120.8 us)
Async XLA Ops:
  4.1 59.8 %all-to-all-start.2 = ((bf16[256,16,256]{0,2,1:T(8,128)(2,1)}), bf16[256,16,256]{0,2,1:T(8,128)(2,1)S(1)}, u32[]{:S(2)}, u32[]{:S(2)}) async-start(bf16[256,16,256]{0,2,1:T(8,128)(2,1)} %bitcast.42), calls=%async_computation.2 | async-start | bytes 4194304 | tf_op jit(solution)/shard_map/all_to_all | solution.py:27
  63.8 54.2 %all-to-all-start = ((bf16[256,16,256]{0,2,1:T(8,128)(2,1)}), bf16[256,16,256]{0,2,1:T(8,128)(2,1)}, u32[]{:S(2)}, u32[]{:S(2)}) async-start(bf16[256,16,256]{0,2,1:T(8,128)(2,1)} %bitcast.41), calls=%async_computation | async-start | bytes 4194304 | tf_op jit(solution)/shard_map/all_to_all | solution.py:28
  118.0 54.2 %all-to-all-start.1 = ((bf16[256,16,256]{0,2,1:T(8,128)(2,1)}), bf16[256,16,256]{0,2,1:T(8,128)(2,1)}, u32[]{:S(2)}, u32[]{:S(2)}) async-start(bf16[256,16,256]{0,2,1:T(8,128)(2,1)} %bitcast.40), calls=%async_computation.1 | async-start | bytes 4194304 | tf_op jit(solution)/shard_map/all_to_all | solution.py:26
  124.8 52.6 %collective-permute-start.1 = (bf16[4096,256]{1,0:T(8,128)(2,1)}, bf16[4096,256]{1,0:T(8,128)(2,1)}, u32[]{:S(2)}, u32[]{:S(2)}) collective-permute-start(bf16[4096,256]{1,0:T(8,128)(2,1)} %bitcast.50), channel_id=1, source_target_pairs={{0,16},{16,32},{32,48},{48,64},{64,80},{80,96},{96,112},{112,128},... | collective-permute-start | bytes 6291464 | tf_op jit(solution)/shard_map/ppermute | solution.py:13
  130.7 65.5 %collective-permute-start = (bf16[4096,256]{1,0:T(8,128)(2,1)}, bf16[4096,256]{1,0:T(8,128)(2,1)}, u32[]{:S(2)}, u32[]{:S(2)}) collective-permute-start(bf16[4096,256]{1,0:T(8,128)(2,1)} %bitcast.49), channel_id=1, source_target_pairs={{0,16},{16,32},{32,48},{48,64},{64,80},{80,96},{96,112},{112,128},... | collective-permute-start | bytes 6291464 | tf_op jit(solution)/shard_map/ppermute | solution.py:13
  141.1 4.3 %copy-start = (bf16[16,256,256]{1,0,2:T(8,128)(2,1)S(1)}, bf16[16,256,256]{1,0,2:T(8,128)(2,1)}, u32[]{:S(2)}) copy-start(bf16[16,256,256]{1,0,2:T(8,128)(2,1)} %copy.45) | copy-start | bytes 6291460
  179.4 21.3 %copy-start.1 = (bf16[4096,2,128]{0,2,1:T(8,128)(2,1)S(1)}, bf16[4096,2,128]{0,2,1:T(8,128)(2,1)}, u32[]{:S(2)}) copy-start(bf16[4096,2,128]{0,2,1:T(8,128)(2,1)} %concatenate.17) | copy-start | bytes 6291460
where the time goes:
time: 403 us; the launch traced here: 401 us
  waiting for transfers between devices  133 us (33%)
  local copies, waits for them, and re-layouts  67.8 us (17%)
  matrix products  67.8 us (17%)
  blocking collectives  57.8 us (14%)
  other arithmetic  45.4 us (11%)
  starting transfers between devices  23.8 us (6%)
  loops' own time  5.49 us (1%)
    all_to_all x1, blocking collectives, shards(): lax.all_to_all(result, 'uly', split_axis=0, concat_axis=1, tiled=True)  57.8 us
    all_to_all x1, waiting for transfers between devices, shards(): lax.all_to_all(keys, 'uly', split_axis=1, concat_axis=0, tiled=True)  46.5 us
    all_to_all x1, waiting for transfers between devices, shards(): lax.all_to_all(values, 'uly', split_axis=1, concat_axis=0, tiled=True)  45.6 us
    dot_general x8, matrix products, attend_span(): jnp.einsum('hqk,khd->qhd', weights, value_rows, preferred_element_type=jn...  37 us
    dot_general x8, matrix products, attend_span(): jnp.einsum('qhd,khd->hqk', query_rows, key_rows, preferred_element_type=j...  30.8 us
    reduce_sum x8, other arithmetic, attend_span(): totals = jnp.sum(probs, axis=-1)  25 us
    all_to_all x1, waiting for transfers between devices, shards(): lax.all_to_all(queries, 'uly', split_axis=1, concat_axis=0, tiled=True)  24.5 us
    ppermute x2, waiting for transfers between devices, shifted(): return lax.ppermute(block, axis, route)  16.7 us
  transfers between devices with their start and end apart: 5, of which 4 were waited for; matrix products, arithmetic and copies ran while one was open for 9% of the time, Pallas kernels for 0%

commit v1 on v0

--- a/solution.py
+++ b/solution.py
@@ -23,7 +23,12 @@
     window = stretch_len // 2
     qblock = min(512, stretch_len)
     query_stretch, key_stretch, value_stretch = (
-        lax.all_to_all(queries, "uly", split_axis=1, concat_axis=0, tiled=True),
+        jnp.concatenate(
+            lax.all_to_all(
+                jnp.stack(jnp.split(queries, lax.axis_size("uly"), axis=1)), "uly", 0, 0
+            ),
+            axis=0,
+        ),
         lax.all_to_all(keys, "uly", split_axis=1, concat_axis=0, tiled=True),
         lax.all_to_all(values, "uly", split_axis=1, concat_axis=0, tiled=True),
     )

time: 403 us -> 411 us (1.020)
  local copies, waits for them, and re-layouts: 67.8 us -> 96.9 us
  waiting for transfers between devices: 133 us -> 113 us
    all_to_all x1, waiting for transfers between devices: 45.6 us -> 24.6 us  [shards(): lax.all_to_all(values, 'uly', split_axis=1, concat_axis=0, tiled=True)]
    unnamed x7 -> x21, local copies, waits for them, and re-layouts: 12.2 us -> 31.7 us
    dynamic_slice x0 -> x8, local copies, waits for them, and re-layouts: none -> 9.1 us  [attend_block(): query_rows = lax.dynamic_slice_in_dim(query_all, first, qblock, 0)]
    another operation x0 -> x2, local copies, waits for them, and re-layouts: none -> 5.6 us  [the longest x1 4.03 us: shards(): query_all = query_stretch.reshape(stretch_len, group_heads, HEAD_DIM)]
  transfers between devices with their start and end apart: 5 -> 5, of which waited for: 4 -> 4; matrix products, arithmetic and copies ran while one was open for 9% -> 13% of each run, Pallas kernels for 0% -> 0%
where the time goes in v1:
time: 411 us; the launch traced here: 409 us
  waiting for transfers between devices  113 us (27%)
  local copies, waits for them, and re-layouts  96.9 us (24%)
  matrix products  66.1 us (16%)
  blocking collectives  57.8 us (14%)
  other arithmetic  45.4 us (11%)
  starting transfers between devices  24 us (6%)
  loops' own time  5.51 us (1%)
    all_to_all x1, blocking collectives, shards(): lax.all_to_all(result, 'uly', split_axis=0, concat_axis=1, tiled=True)  57.8 us
    all_to_all x1, waiting for transfers between devices, shards(): lax.all_to_all(keys, 'uly', split_axis=1, concat_axis=0, tiled=True)  46.5 us
    dot_general x8, matrix products, attend_span(): jnp.einsum('hqk,khd->qhd', weights, value_rows, preferred_element_type=jn...  37 us
    unnamed x21, local copies, waits for them, and re-layouts  31.7 us
    dot_general x8, matrix products, attend_span(): jnp.einsum('qhd,khd->hqk', query_rows, key_rows, preferred_element_type=j...  29.2 us
    reduce_sum x8, other arithmetic, attend_span(): totals = jnp.sum(probs, axis=-1)  25 us
    all_to_all x1, waiting for transfers between devices, shards(): lax.all_to_all(values, 'uly', split_axis=1, concat_axis=0, tiled=True)  24.6 us
    all_to_all x1, waiting for transfers between devices, shards(): lax.all_to_all(jnp.stack(jnp.split(queries, lax.axis_size('uly'), axis=1)...  24.3 us
  transfers between devices with their start and end apart: 5, of which 4 were waited for; matrix products, arithmetic and copies ran while one was open for 13% of the time, Pallas kernels for 0%

profile of v1, /device:TPU:12, one launch (start us, length us, event | category | flops | bytes accessed | tf_op | source)
XLA Modules:
  0.0 409.0 jit_solution(11568504870091706821)
XLA Ops:
  0.0 4.1 copy.40
  4.1 9.2 %all-to-all-start.2 = ((bf16[256,16,256]{0,2,1:T(8,128)(2,1)}), bf16[256,16,256]{0,2,1:T(8,128)(2,1)S(1)}, u32[]{:S(2)}, u32[]{:S(2)}) async-start(bf16[256,16,256]{0,2,1:T(8,128)(2,1)} %bitcast.69), calls=%async_computation.2 | async-start | bytes 4194304 | tf_op jit(solution)/shard_map/all_to_all | solution.py:32
  13.3 4.1 copy.35
  17.4 46.5 %all-to-all-done.2 = bf16[256,16,256]{0,2,1:T(8,128)(2,1)S(1)} async-done(((bf16[256,16,256]{0,2,1:T(8,128)(2,1)}), bf16[256,16,256]{0,2,1:T(8,128)(2,1)S(1)}, u32[]{:S(2)}, u32[]{:S(2)}) %all-to-all-start.2) | async-done | bytes 2097184 | tf_op jit(solution)/shard_map/all_to_all | solution.py:32
  63.8 4.4 %all-to-all-start = ((bf16[256,16,256]{0,2,1:T(8,128)(2,1)}), bf16[256,16,256]{0,2,1:T(8,128)(2,1)}, u32[]{:S(2)}, u32[]{:S(2)}) async-start(bf16[256,16,256]{0,2,1:T(8,128)(2,1)} %bitcast.68), calls=%async_computation | async-start | bytes 4194304 | tf_op jit(solution)/shard_map/all_to_all | solution.py:33
  93.4 24.6 %all-to-all-done = bf16[256,16,256]{0,2,1:T(8,128)(2,1)} async-done(((bf16[256,16,256]{0,2,1:T(8,128)(2,1)}), bf16[256,16,256]{0,2,1:T(8,128)(2,1)}, u32[]{:S(2)}, u32[]{:S(2)}) %all-to-all-start) | async-done | bytes 2097184 | tf_op jit(solution)/shard_map/all_to_all | solution.py:33
  118.0 4.4 %all-to-all-start.1 = ((bf16[16,256,256]{2,1,0:T(8,128)(2,1)}), bf16[16,256,256]{2,1,0:T(8,128)(2,1)}, u32[]{:S(2)}, u32[]{:S(2)}) async-start(bf16[16,256,256]{2,1,0:T(8,128)(2,1)} %bitcast_dynamic-update-slice_fusion), calls=%async_computation.1 | async-start | bytes 4194304 | tf_op jit(solution)/shard_map/all_to_all | solution.py:27
  137.2 4.1 copy.37
  141.3 4.3 %concatenate.17 = bf16[4096,2,128]{0,2,1:T(8,128)(2,1)} reshape(bf16[16,256,256]{1,0,2:T(8,128)(2,1)} %copy.37) | data formatting | bytes 4194304 | tf_op jit(solution)/shard_map/concatenate | solution.py:42
  148.0 24.3 %all-to-all-done.1 = bf16[16,256,256]{2,1,0:T(8,128)(2,1)} async-done(((bf16[16,256,256]{2,1,0:T(8,128)(2,1)}), bf16[16,256,256]{2,1,0:T(8,128)(2,1)}, u32[]{:S(2)}, u32[]{:S(2)}) %all-to-all-start.1) | async-done | bytes 2097184 | tf_op jit(solution)/shard_map/all_to_all | solution.py:27
  172.2 4.0 reshape.124
  178.2 17.9 %collective-permute-done = bf16[4096,256]{1,0:T(8,128)(2,1)} collective-permute-done((bf16[4096,256]{1,0:T(8,128)(2,1)}, bf16[4096,256]{1,0:T(8,128)(2,1)}, u32[]{:S(2)}, u32[]{:S(2)}) %collective-permute-start) | collective-permute-done | bytes 2097184 | tf_op jit(solution)/shard_map/ppermute | solution.py:13
  200.7 4.3 %pad_maximum_fusion = (bf16[6144,2,128]{0,2,1:T(8,128)(2,1)}, bf16[6144,2,128]{0,2,1:T(8,128)(2,1)}) fusion(bf16[4096,2,128]{0,2,1:T(8,128)(2,1)S(1)} %copy-done.1, bf16[2048,2,128]{0,2,1:T(8,128)(2,1)} %bitcast.74, bf16[4096,2,128]{0,2,1:T(8,128)(2,1)} %concatenate.20, bf16[2048,2,128]{0,2,1:T(8,128)(2,1)S(1)} %bitcast.73), kind=kLoop, calls=%fused_computation.24 | loop fusion | flops 12582912 | bytes 12582912 | tf_op jit(solution)/shard_map/concatenate | solution.py:42
  205.0 139.8 %while.13 = (s32[]{:T(128)}, bf16[8,512,256]{2,1,0:T(8,128)(2,1)}, s32[8]{0:T(128)S(1)}, bf16[6144,2,128]{0,2,1:T(8,128)(2,1)}, s32[]{:T(128)}, /*index=5*/s32[4...) while((s32[]{:T(128)}, bf16[8,512,256]{2,1,0:T(8,128)(2,1)}, ...), condition=%wide.region_3.4_spmd, body=%wide.region_0.3_spmd.sunk | while | flops 1377830400 | bytes 41474824 | solution.py:78
  217.0 4.6 %fusion.38 = bf16[512,2,128]{0,2,1:T(8,128)(2,1)S(1)} fusion(f32[2,512,2560]{2,1,0:T(8,128)S(1)} %get-tuple-element.238, f32[2,512]{1,0:T(2,128)S(1)} %get-tuple-element.239, pred[512,2560]{1,0:T(8,128)(4,1)S(1)} %compare_and_fusion.2, bf16[6144,2,128]{0,2,1:T(8,128)(2,1)} %get-tuple-element.271, s32[]{:T(128)S(6)} %select_n.49, ...), kind=kOutput, calls=%fused_computation.13.clone.1 | convolution fusion | flops 681836544 | bytes 13377540 | tf_op jit(solution)/shard_map/while/body/eval_jaxpr/hqk,khd->qhd/dot_general | solution.py:68
  234.4 4.6 %fusion.38 = bf16[512,2,128]{0,2,1:T(8,128)(2,1)S(1)} fusion(f32[2,512,2560]{2,1,0:T(8,128)S(1)} %get-tuple-element.238, f32[2,512]{1,0:T(2,128)S(1)} %get-tuple-element.239, pred[512,2560]{1,0:T(8,128)(4,1)S(1)} %compare_and_fusion.2, bf16[6144,2,128]{0,2,1:T(8,128)(2,1)} %get-tuple-element.271, s32[]{:T(128)S(6)} %select_n.49, ...), kind=kOutput, calls=%fused_computation.13.clone.1 | convolution fusion | flops 681836544 | bytes 13377540 | tf_op jit(solution)/shard_map/while/body/eval_jaxpr/hqk,khd->qhd/dot_general | solution.py:68
  251.9 4.6 %fusion.38 = bf16[512,2,128]{0,2,1:T(8,128)(2,1)S(1)} fusion(f32[2,512,2560]{2,1,0:T(8,128)S(1)} %get-tuple-element.238, f32[2,512]{1,0:T(2,128)S(1)} %get-tuple-element.239, pred[512,2560]{1,0:T(8,128)(4,1)S(1)} %compare_and_fusion.2, bf16[6144,2,128]{0,2,1:T(8,128)(2,1)} %get-tuple-element.271, s32[]{:T(128)S(6)} %select_n.49, ...), kind=kOutput, calls=%fused_computation.13.clone.1 | convolution fusion | flops 681836544 | bytes 13377540 | tf_op jit(solution)/shard_map/while/body/eval_jaxpr/hqk,khd->qhd/dot_general | solution.py:68
  269.4 4.6 %fusion.38 = bf16[512,2,128]{0,2,1:T(8,128)(2,1)S(1)} fusion(f32[2,512,2560]{2,1,0:T(8,128)S(1)} %get-tuple-element.238, f32[2,512]{1,0:T(2,128)S(1)} %get-tuple-element.239, pred[512,2560]{1,0:T(8,128)(4,1)S(1)} %compare_and_fusion.2, bf16[6144,2,128]{0,2,1:T(8,128)(2,1)} %get-tuple-element.271, s32[]{:T(128)S(6)} %select_n.49, ...), kind=kOutput, calls=%fused_computation.13.clone.1 | convolution fusion | flops 681836544 | bytes 13377540 | tf_op jit(solution)/shard_map/while/body/eval_jaxpr/hqk,khd->qhd/dot_general | solution.py:68
  286.9 4.6 %fusion.38 = bf16[512,2,128]{0,2,1:T(8,128)(2,1)S(1)} fusion(f32[2,512,2560]{2,1,0:T(8,128)S(1)} %get-tuple-element.238, f32[2,512]{1,0:T(2,128)S(1)} %get-tuple-element.239, pred[512,2560]{1,0:T(8,128)(4,1)S(1)} %compare_and_fusion.2, bf16[6144,2,128]{0,2,1:T(8,128)(2,1)} %get-tuple-element.271, s32[]{:T(128)S(6)} %select_n.49, ...), kind=kOutput, calls=%fused_computation.13.clone.1 | convolution fusion | flops 681836544 | bytes 13377540 | tf_op jit(solution)/shard_map/while/body/eval_jaxpr/hqk,khd->qhd/dot_general | solution.py:68
  304.3 4.6 %fusion.38 = bf16[512,2,128]{0,2,1:T(8,128)(2,1)S(1)} fusion(f32[2,512,2560]{2,1,0:T(8,128)S(1)} %get-tuple-element.238, f32[2,512]{1,0:T(2,128)S(1)} %get-tuple-element.239, pred[512,2560]{1,0:T(8,128)(4,1)S(1)} %compare_and_fusion.2, bf16[6144,2,128]{0,2,1:T(8,128)(2,1)} %get-tuple-element.271, s32[]{:T(128)S(6)} %select_n.49, ...), kind=kOutput, calls=%fused_computation.13.clone.1 | convolution fusion | flops 681836544 | bytes 13377540 | tf_op jit(solution)/shard_map/while/body/eval_jaxpr/hqk,khd->qhd/dot_general | solution.py:68
  321.8 4.6 %fusion.38 = bf16[512,2,128]{0,2,1:T(8,128)(2,1)S(1)} fusion(f32[2,512,2560]{2,1,0:T(8,128)S(1)} %get-tuple-element.238, f32[2,512]{1,0:T(2,128)S(1)} %get-tuple-element.239, pred[512,2560]{1,0:T(8,128)(4,1)S(1)} %compare_and_fusion.2, bf16[6144,2,128]{0,2,1:T(8,128)(2,1)} %get-tuple-element.271, s32[]{:T(128)S(6)} %select_n.49, ...), kind=kOutput, calls=%fused_computation.13.clone.1 | convolution fusion | flops 681836544 | bytes 13377540 | tf_op jit(solution)/shard_map/while/body/eval_jaxpr/hqk,khd->qhd/dot_general | solution.py:68
  339.3 4.6 %fusion.38 = bf16[512,2,128]{0,2,1:T(8,128)(2,1)S(1)} fusion(f32[2,512,2560]{2,1,0:T(8,128)S(1)} %get-tuple-element.238, f32[2,512]{1,0:T(2,128)S(1)} %get-tuple-element.239, pred[512,2560]{1,0:T(8,128)(4,1)S(1)} %compare_and_fusion.2, bf16[6144,2,128]{0,2,1:T(8,128)(2,1)} %get-tuple-element.271, s32[]{:T(128)S(6)} %select_n.49, ...), kind=kOutput, calls=%fused_computation.13.clone.1 | convolution fusion | flops 681836544 | bytes 13377540 | tf_op jit(solution)/shard_map/while/body/eval_jaxpr/hqk,khd->qhd/dot_general | solution.py:68
  344.8 57.8 %all_to_all.62 = bf16[16,256,256]{2,1,0:T(8,128)(2,1)S(1)} all-to-all(bf16[16,256,256]{2,1,0:T(8,128)(2,1)} %bitcast.75), channel_id=1, replica_groups=mesh['blk'=16,'uly'=16] {'uly'}, dimensions={0} | all-to-all | bytes 4194304 | tf_op jit(solution)/shard_map/all_to_all | solution.py:80
  404.9 4.1 copy.48
  (114 shorter events, 148.4 us)
Async XLA Ops:
  4.1 59.8 %all-to-all-start.2 = ((bf16[256,16,256]{0,2,1:T(8,128)(2,1)}), bf16[256,16,256]{0,2,1:T(8,128)(2,1)S(1)}, u32[]{:S(2)}, u32[]{:S(2)}) async-start(bf16[256,16,256]{0,2,1:T(8,128)(2,1)} %bitcast.69), calls=%async_computation.2 | async-start | bytes 4194304 | tf_op jit(solution)/shard_map/all_to_all | solution.py:32
  63.8 54.2 %all-to-all-start = ((bf16[256,16,256]{0,2,1:T(8,128)(2,1)}), bf16[256,16,256]{0,2,1:T(8,128)(2,1)}, u32[]{:S(2)}, u32[]{:S(2)}) async-start(bf16[256,16,256]{0,2,1:T(8,128)(2,1)} %bitcast.68), calls=%async_computation | async-start | bytes 4194304 | tf_op jit(solution)/shard_map/all_to_all | solution.py:33
  118.0 54.2 %all-to-all-start.1 = ((bf16[16,256,256]{2,1,0:T(8,128)(2,1)}), bf16[16,256,256]{2,1,0:T(8,128)(2,1)}, u32[]{:S(2)}, u32[]{:S(2)}) async-start(bf16[16,256,256]{2,1,0:T(8,128)(2,1)} %bitcast_dynamic-update-slice_fusion), calls=%async_computation.1 | async-start | bytes 4194304 | tf_op jit(solution)/shard_map/all_to_all | solution.py:27
  124.8 51.4 %collective-permute-start.1 = (bf16[4096,256]{1,0:T(8,128)(2,1)}, bf16[4096,256]{1,0:T(8,128)(2,1)}, u32[]{:S(2)}, u32[]{:S(2)}) collective-permute-start(bf16[4096,256]{1,0:T(8,128)(2,1)} %bitcast.77), channel_id=1, source_target_pairs={{0,16},{16,32},{32,48},{48,64},{64,80},{80,96},{96,112},{112,128},... | collective-permute-start | bytes 6291464 | tf_op jit(solution)/shard_map/ppermute | solution.py:13
  130.7 65.5 %collective-permute-start = (bf16[4096,256]{1,0:T(8,128)(2,1)}, bf16[4096,256]{1,0:T(8,128)(2,1)}, u32[]{:S(2)}, u32[]{:S(2)}) collective-permute-start(bf16[4096,256]{1,0:T(8,128)(2,1)} %bitcast.76), channel_id=1, source_target_pairs={{0,16},{16,32},{32,48},{48,64},{64,80},{80,96},{96,112},{112,128},... | collective-permute-start | bytes 6291464 | tf_op jit(solution)/shard_map/ppermute | solution.py:13
  141.3 4.4 %copy-start = (bf16[16,256,256]{1,0,2:T(8,128)(2,1)S(1)}, bf16[16,256,256]{1,0,2:T(8,128)(2,1)}, u32[]{:S(2)}) copy-start(bf16[16,256,256]{1,0,2:T(8,128)(2,1)} %copy.43) | copy-start | bytes 6291460
  178.2 22.5 %copy-start.1 = (bf16[4096,2,128]{0,2,1:T(8,128)(2,1)S(1)}, bf16[4096,2,128]{0,2,1:T(8,128)(2,1)}, u32[]{:S(2)}) copy-start(bf16[4096,2,128]{0,2,1:T(8,128)(2,1)} %concatenate.17) | copy-start | bytes 6291460
